TPU v7x, 32 devices: a whole 2x2x4 slice. The times are simulated.
32 devices in a mesh: view: 4 (over x, core), patch: 8 (over z, y).
Axes of the slice: x: 2, y: 2, z: 4, core: 2. Of those that a mesh axis runs over, the one named last changes fastest.
Arguments:
- queries: bfloat16 [4096, 768], P(('view', 'patch')), may hold values from -6 to 6
- key_rows: bfloat16 [4096, 768], P(('view', 'patch')), may hold values from -6 to 6
- value_rows: bfloat16 [4096, 768], P(('view', 'patch')), may hold values from -6 to 6
- step_rates: float32 [4096, 4], P(('view', 'patch')), may hold values from 0.5 to 18, as said below
- fast_init: float32 [192, 4608], replicated, may hold values from -2.598076 to 2.598076
- out_grad: bfloat16 [4096, 768], P(('view', 'patch')), may hold values from -6 to 6
Outputs:
- query_grad: bfloat16 [4096, 768], P(('view', 'patch'))
- key_grad: bfloat16 [4096, 768], P(('view', 'patch'))
- value_grad: bfloat16 [4096, 768], P(('view', 'patch'))
- rate_grad: float32 [4096, 4], P(('view', 'patch'))
- fast_grad: float32 [192, 4608], P(None, ('view', 'patch'))
Inputs may be any that keep to these rules, and one draw needn't show every extreme that they name: `step_rates`: positive learning rates.
All inputs are finite; a program needn't handle non-finite values.
Results may differ from a plain program's by a relative error of at most 0.0023.
Values sent between devices are 32-bit elements; how exact they have to be, the bound alone decides.
No kernel may reach another device: no remote copies, remote signals or barrier semaphores. Data moves between devices by JAX's collectives and lax.ppermute only.
A program may use at most 128 MiB of HBM per device.

v0:
```python
import math

import jax
import jax.numpy as jnp
from jax import lax
from jax.sharding import PartitionSpec as P

highest = lax.Precision.HIGHEST
product_precision = lax.Precision.HIGH
step_size = 0.2
epsilon = 1e-06


def fast_apply(inputs, weights):
    gate_act = jnp.einsum("rhd,dhc->rhc", inputs, weights[:, 0], precision=product_precision)
    up_act = jnp.einsum("rhd,dhc->rhc", inputs, weights[:, 1], precision=product_precision)
    hidden = jax.nn.silu(gate_act) * up_act
    return jnp.einsum("rhc,dhc->rhd", hidden, weights[:, 2], precision=product_precision)


def update_term(key_part, value_part, rate_part, weights):

    def objective(fast):
        return -jnp.sum(rate_part[:, :, None] * value_part * fast_apply(key_part, fast))

    return jax.grad(objective)(weights)


def head_columns(first_col, own_width, heads, hidden_units):
    column_ids = first_col + jnp.arange(own_width, dtype=jnp.int32)
    head_ids = column_ids // hidden_units % heads
    return (head_ids[:, None] == jnp.arange(heads, dtype=jnp.int32)[None, :]).astype(jnp.float32)


def rate_totals(step_rates):
    return lax.psum(jnp.sum(step_rates, 0), ("view", "patch"))


def on_device(queries, key_rows, value_rows, step_rates, fast_init, out_grad):
    row_count = queries.shape[0]
    head_dim, columns = fast_init.shape
    heads = step_rates.shape[1]
    hidden_units = columns // (3 * heads)
    devices = lax.axis_size("view") * lax.axis_size("patch")
    coefficient = step_size * math.sqrt(row_count * devices)
    share = columns // devices
    my_first = lax.axis_index(("view", "patch")) * share

    def to_heads(tensor):
        return tensor.astype(jnp.float32).reshape(row_count, heads, head_dim)

    def from_heads(tensor):
        return tensor.reshape(row_count, heads * head_dim).astype(jnp.bfloat16)

    weights = fast_init.reshape(head_dim, 3, heads, hidden_units)
    totals = rate_totals(step_rates)
    rate_scale = coefficient / totals
    partial_value, pull_update = jax.vjp(
        update_term, to_heads(key_rows), to_heads(value_rows), step_rates, weights
    )
    flat_terms = partial_value.reshape(head_dim, columns)
    first_col = 0
    summed = lax.psum(flat_terms, ("view", "patch"))
    owner_map = head_columns(first_col, columns, heads, hidden_units)
    col_scale = jnp.dot(owner_map, rate_scale, precision=highest)
    grad_cols = summed * col_scale[None, :]
    moved = fast_init - grad_cols
    init_norm = jnp.sqrt(jnp.sum(fast_init * fast_init, 0) + epsilon)
    inverse = lax.rsqrt(jnp.sum(moved * moved, 0) + epsilon)
    col_ratio = init_norm * inverse
    renormed = moved * col_ratio
    _, pull_apply = jax.vjp(
        fast_apply, to_heads(queries), renormed.reshape(head_dim, 3, heads, hidden_units)
    )
    query_part, new_part = pull_apply(to_heads(out_grad))
    flat_new = new_part.reshape(head_dim, columns)
    d_new = lax.psum(flat_new, ("view", "patch"))
    column_dots = jnp.sum(d_new * moved, 0)
    d_moved = d_new * col_ratio - moved * (column_dots * init_norm * inverse * inverse * inverse)
    direct = d_moved + fast_init * (column_dots * inverse / init_norm)
    d_update = -d_moved
    head_part = jnp.dot(jnp.sum(d_update * grad_cols, 0), owner_map, precision=highest)
    d_totals = -head_part / totals
    d_terms = d_update * col_scale[None, :]
    key_part, value_part, rate_part, fast_part = pull_update(
        d_terms.reshape(head_dim, 3, heads, hidden_units)
    )
    rate_grad = rate_part + d_totals[None, :]
    second = lax.psum_scatter(
        fast_part.reshape(head_dim, columns), ("view", "patch"), scatter_dimension=1, tiled=True
    )
    direct_own = lax.dynamic_slice_in_dim(direct, my_first, share, 1)
    fast_grad = (direct_own + second) / math.sqrt(row_count * devices)
    return (
        from_heads(query_part),
        from_heads(key_part),
        from_heads(value_part),
        rate_grad,
        fast_grad,
    )


def solution(mesh):
    return jax.shard_map(
        on_device,
        mesh=mesh,
        in_specs=(
            P(("view", "patch"), None),
            P(("view", "patch"), None),
            P(("view", "patch"), None),
            P(("view", "patch"), None),
            P(),
            P(("view", "patch"), None),
        ),
        out_specs=(
            P(("view", "patch"), None),
            P(("view", "patch"), None),
            P(("view", "patch"), None),
            P(("view", "patch"), None),
            P(None, ("view", "patch")),
        ),
        check_vma=False,
    )
```

profile of v0, /device:TPU:0, one launch (start us, length us, event | category | flops | bytes accessed | tf_op | source)
XLA Modules:
  0.0 485.0 jit_solution(17959862862304572160)
XLA Ops:
  7.2 1.7 copy.90
  9.0 3.3 reshape.112
  12.3 2.1 fusion.77
  14.4 1.1 copy.88
  15.5 2.5 fusion.8
  18.0 1.5 convolution_bitcast_fusion.9
  19.6 1.0 fusion.74
  21.3 0.8 convolution_bitcast_fusion.1
  23.2 2.3 copy.95
  25.4 3.1 reshape.114
  28.7 42.4 %psum.22 = f32[4]{0:T(128)S(1)} all-reduce(f32[4]{0:T(128)S(1)} %get-tuple-element.48), channel_id=1, replica_groups=mesh['view'=4,'patch'=8] {'view','patch'}, use_global_device_ids=true, to_apply=%region_2.3 | all-reduce | flops 4 | bytes 32 | tf_op jit(solution)/shard_map/psum | solution.py:36
  71.1 0.8 copy.99
  71.9 0.8 copy.97
  73.3 0.8 convolution_reduce_fusion
  74.2 97.3 %all-reduce.12.cloned.1.call-done = f32[192,4608]{1,0:T(8,128)} async-done(((f32[192,4608]{1,0:T(8,128)}), f32[192,4608]{1,0:T(8,128)}) %all-reduce.12.cloned.1.call-update) | async-done | bytes 3538960 | tf_op jit(solution)/shard_map/psum | solution.py:63
  171.5 3.9 multiply_reduce_fusion.2
  176.6 2.2 broadcast_multiply_fusion
  178.8 5.2 %reshape.115 = f32[192,3,4,384]{3,2,1,0:T(4,128)} reshape(f32[192,4608]{1,0:T(8,128)} %broadcast_multiply_fusion) | data formatting | bytes 7077888 | tf_op jit(solution)/shard_map/reshape | solution.py:73
  184.0 2.7 fusion.76
  186.7 1.0 fusion.9
  187.7 1.0 fusion.10
  188.9 1.0 fusion.4
  192.5 4.1 copy.102
  196.6 5.4 %reshape.118 = f32[192,4608]{1,0:T(8,128)} reshape(f32[192,3,4,384]{3,2,1,0:T(4,128)} %copy.102) | data formatting | bytes 7077888 | tf_op jit(solution)/shard_map/reshape | solution.py:76
  202.3 138.9 %all-reduce.14.cloned.1.call-done = f32[192,4608]{1,0:T(8,128)} async-done(((f32[192,4608]{1,0:T(8,128)}), f32[192,4608]{1,0:T(8,128)}) %all-reduce.14.cloned.1.call-update) | async-done | bytes 3538960 | tf_op jit(solution)/shard_map/psum | solution.py:77
  341.1 2.5 multiply_reduce_fusion.1
  343.7 2.0 rsqrt_multiply_fusion
  345.7 1.8 multiply_reduce_fusion
  347.5 1.8 copy-done
  349.3 2.1 negate_multiply_fusion
  351.4 3.3 reshape.119
  355.7 1.0 fusion.12
  357.1 0.8 copy-done.44
  358.0 1.1 fusion.29
  359.7 2.0 multiply_add_fusion
  364.0 3.7 copy.122
  367.8 1.2 copy-done.13
  369.4 0.9 fusion.11
  370.9 1.7 fusion.5
  372.6 1.7 copy.110
  375.9 2.4 fusion.13
  378.4 0.8 fusion.3
  380.6 0.8 copy.111
  383.1 0.8 multiply_reduce_fusion.4
  384.0 0.8 copy.112
  386.6 88.4 %reduce-scatter.4.cloned.1.call-done = f32[144,192]{1,0:T(8,128)} async-done(((f32[4608,192]{1,0:T(8,128)}), f32[144,192]{1,0:T(8,128)}) %reduce-scatter.4.cloned.1.call-update) | async-done | bytes 110608
  474.9 1.0 copy.121
  476.0 1.2 fusion.46
  (148 shorter events, 19.0 us)
Async XLA Ops:
  7.2 164.3 %all-reduce.12.cloned.1.call-start = ((), (), s32[]{:S(2)}) async-start(), calls=%async_computation.1 | async-start | bytes 7077888 | tf_op jit(solution)/shard_map/psum | solution.py:63
  15.5 5.9 %copy-start.16 = (f32[128,768]{0,1:T(8,128)}, f32[128,768]{0,1:T(8,128)S(1)}, u32[]{:S(2)}) copy-start(f32[128,768]{0,1:T(8,128)S(1)} %copy.88) | copy-start | bytes 1179652
  15.5 2.5 copy-start.3
  15.5 2.5 copy-start.60
  18.0 3.3 copy-start.25
  18.0 1.5 copy-start.6
  18.0 1.5 copy-start.8
  20.6 1.5 copy-start.43
  20.6 1.5 copy-start.46
  20.7 1.5 copy-start.48
  28.5 42.6 %copy-start.50 = (bf16[128,768]{1,0:T(8,128)(2,1)S(1)}, bf16[128,768]{1,0:T(8,128)(2,1)}, u32[]{:S(2)}) copy-start(bf16[128,768]{1,0:T(8,128)(2,1)} %param.11) | copy-start | bytes 589828
  28.5 43.4 %copy-start.51 = (bf16[128,768]{1,0:T(8,128)(2,1)S(1)}, bf16[128,768]{1,0:T(8,128)(2,1)}, u32[]{:S(2)}) copy-start(bf16[128,768]{1,0:T(8,128)(2,1)} %param.6) | copy-start | bytes 589828
  28.5 312.6 %all-reduce.14.cloned.1.call-start = ((), (), s32[]{:S(2)}) async-start(), calls=%async_computation.2 | async-start | bytes 7077888 | tf_op jit(solution)/shard_map/psum | solution.py:77
  184.0 2.7 copy-start.31
  186.6 2.2 copy-start.10
  186.6 2.2 copy-start.12
  187.7 3.9 copy-start.37
  188.8 2.8 copy-start.39
  202.0 272.9 %reduce-scatter.4.cloned.1.call-start = ((), (), s32[]{:S(2)}) async-start(), calls=%async_computation.3 | async-start | bytes 4866048
  341.1 4.5 copy-start.1
  341.1 4.5 copy-start.2
  341.1 4.5 copy-start.52
  341.1 4.5 copy-start.54
  347.5 1.8 copy-start
  355.4 3.7 copy-start.14
  355.4 3.7 copy-start.34
  355.4 3.7 copy-start.32
  355.4 1.7 copy-start.26
  355.4 2.6 copy-start.44
  358.0 1.5 copy-start.47
  358.0 1.7 copy-start.49
  359.1 4.0 copy-start.23
  361.7 1.4 copy-start.19
  367.7 1.5 copy-start.38
  367.7 1.7 copy-start.42
  369.4 1.5 copy-start.40
  370.9 3.4 copy-start.7
  370.9 3.4 copy-start.22
  374.3 1.3 copy-start.15
  374.3 1.6 copy-start.45
  375.9 2.4 copy-start.30
  375.9 2.4 copy-start.35
  378.3 1.5 copy-start.20
  379.9 1.6 copy-start.4
  379.9 1.6 copy-start.24
  381.5 1.7 copy-start.33
  383.1 1.7 copy-start.57
  383.1 2.5 copy-start.59
  (16 other events, 16.0 us)
Sparse Core Ops, SparseCore 0:
  28.6 142.7 all-reduce.11
  202.1 138.9 all-reduce.13
  367.9 107.0 reduce-scatter.3
where the time goes:
time: 493 us; the launch traced here: 485 us
  waiting for transfers between devices  325 us (66%)
  local copies, waits for them, and re-layouts  57.2 us (12%)
  blocking collectives  42.4 us (9%)
  matrix products  28.1 us (6%)
  other arithmetic  17.3 us (4%)
  between operations  15 us (3%)
    psum x1, waiting for transfers between devices, on_device(): d_new = lax.psum(flat_new, ('view', 'patch'))  139 us
    psum x1, waiting for transfers between devices, on_device(): summed = lax.psum(flat_terms, ('view', 'patch'))  97.3 us
    unnamed x4, waiting for transfers between devices  88.4 us
    psum x1, blocking collectives, rate_totals(): return lax.psum(jnp.sum(step_rates, 0), ('view', 'patch'))  42.4 us
    unnamed x131, local copies, waits for them, and re-layouts  23.4 us
    dot_general x9, matrix products, fast_apply(): jnp.einsum('rhd,dhc->rhc', inputs, weights[:, 0], precision=product_preci...  9.98 us
  transfers between devices with their start and end apart: 3, of which 3 were waited for; matrix products, arithmetic and copies ran while one was open for 3% of the time, Pallas kernels for 0%

commit v1 on v0

v1 whole, which is shorter than its diff:
```python
import functools
import math

import jax
import jax.numpy as jnp
from jax import lax
from jax.experimental import pallas as pl
from jax.experimental.pallas import tpu as pltpu
from jax.sharding import PartitionSpec as P

AXES = ("view", "patch")
step_size = 0.2
epsilon = 1e-06
F32, BF16 = jnp.float32, jnp.bfloat16
LANES, SUBLANES = 128, 8


class Layout:
    def __init__(self, views, patches, heads, hidden, head_dim):
        self.heads, self.head_dim, self.hidden = heads, head_dim, hidden
        self.cores = 2 if views % 2 == 0 else 1
        self.patches, self.devices = patches, views * patches
        self.sub = patches // heads
        self.plane = (views // self.cores) * self.sub
        self.half = hidden // self.cores
        self.slot = self.half // self.plane
        self.pow2 = self.plane & (self.plane - 1) == 0
        rows = 3 * self.slot
        self.packed = head_dim == LANES + LANES // 2 and rows % (4 * SUBLANES) in (0, 2 * SUBLANES)

    def place(self, device):
        view, patch = divmod(device, self.patches)
        outer, core = divmod(view, self.cores)
        head, sub = divmod(patch, self.sub)
        return outer * self.sub + sub, core, head

    def device(self, member, core, head):
        outer, sub = divmod(member, self.sub)
        return (outer * self.cores + core) * self.patches + head * self.sub + sub

    def target(self, member, step):
        return member ^ step if self.pow2 else (member + step) % self.plane

    def origin(self, member, step):
        return member ^ step if self.pow2 else (member - step) % self.plane

    def perm(self, move):
        return [(i, self.device(*move(*self.place(i)))) for i in range(self.devices)]

    def core_perm(self):
        return self.perm(lambda j, c, h: (j, (c + 1) % self.cores, h))

    def head_perm(self, shift):
        return self.perm(lambda j, c, h: (j, c, (h + shift) % self.heads))

    def scatter_perm(self, step):
        return self.perm(lambda j, c, h: (self.target(j, step), c, h))

    def gather_perm(self, step):
        return self.perm(lambda j, c, h: (self.origin(j, step), c, h))

    def owner_rounds(self):
        count = self.devices
        edges = []
        for i in range(count):
            j, c, h = self.place(i)
            for m in range(3):
                piece = (m * self.heads + h) * self.cores * self.plane + c * self.plane + j
                edges.append((i, piece // 3, m, piece % 3))
        left, rounds = list(edges), []
        for _ in range(3):
            out_edges = [[] for _ in range(count)]
            for edge in left:
                out_edges[edge[0]].append(edge)
            match = {}

            def place_one(i, seen):
                for edge in out_edges[i]:
                    if edge[1] in seen:
                        continue
                    seen.add(edge[1])
                    if edge[1] not in match or place_one(match[edge[1]][0], seen):
                        match[edge[1]] = edge
                        return True
                return False

            for i in range(count):
                place_one(i, set())
            chosen = sorted(match.values())
            rounds.append(chosen)
            left = [edge for edge in left if edge not in match.values()]
        return rounds


def split(lay, x):
    if not lay.packed:
        return (x,)
    high = x.astype(BF16)
    return high, (x - high.astype(F32)).astype(BF16)


def dot(a, b, dims, precision=None):
    return lax.dot_general(
        a, b, (dims, ((), ())), precision=precision, preferred_element_type=F32
    )


NN, NT = ((1,), (0,)), ((1,), (1,))


def dot_left(parts, exact, dims):
    if len(parts) == 1:
        return dot(parts[0], exact, dims, lax.Precision.HIGH)
    return dot(parts[0], exact, dims) + dot(parts[1], exact, dims)


def dot_both(a, b, dims):
    if len(a) == 1:
        return dot(a[0], b[0], dims, lax.Precision.HIGH)
    return dot(a[0], b[0], dims) + (dot(a[0], b[1], dims) + dot(a[1], b[0], dims))


def gates(act):
    sig = 1.0 / (1.0 + jnp.exp(-act))
    silu = act * sig
    rest = 1.0 - sig
    return sig, silu, rest, sig + silu * rest


def cat(parts, axis):
    return jnp.concatenate(parts, axis)


def pack(lay, body, extra):
    if not lay.packed:
        return cat([body, jnp.broadcast_to(extra, (SUBLANES, lay.head_dim))], 0)
    rows = body.shape[0]
    tail = body[:, LANES:]
    tail = cat([tail[: rows // 2], tail[rows // 2 :]], 1)
    return cat([body[:, :LANES], tail, jnp.broadcast_to(extra, (SUBLANES, LANES))], 0)


def unpack(lay, payload):
    rows = 3 * lay.slot
    if not lay.packed:
        return payload[:rows], payload[rows : rows + 1, :1]
    tail = payload[rows : rows + rows // 2]
    half = LANES // 2
    tail = cat([tail[:, :half], tail[:, half:]], 0)
    return cat([payload[:rows], tail], 1), payload[rows + rows // 2 : rows + rows // 2 + 1, :1]


def pack_all(lay, grads, extra):
    outs = []
    for step in range(lay.plane):
        take = slice(step * lay.slot, (step + 1) * lay.slot)
        outs.append(pack(lay, cat([g[take] for g in grads], 0), extra))
    return outs


def unpack_all(lay, payloads):
    bodies = [unpack(lay, p)[0] for p in payloads]
    slot = lay.slot
    return [cat([b[m * slot : (m + 1) * slot] for b in bodies], 0) for m in range(3)]


def select_heads(lay, pieces, head_ids, shift):
    wanted = lax.rem(head_ids[0:1, :] + shift, lay.heads)
    result = pieces[0]
    for h in range(1, lay.heads):
        result = jnp.where(wanted == h, pieces[h], result)
    return result


def spread_rows(lay, with_rates, first, second, *rest):
    dim = lay.head_dim
    head_ids = rest[-1]
    turned = [x.astype(F32).T for x in (first, second)]
    pieces = [[t[h * dim : (h + 1) * dim] for h in range(lay.heads)] for t in turned]
    if with_rates:
        rates = rest[0]
        rows = rates.shape[0]
        rates = cat([rates, jnp.zeros((rows, LANES - lay.heads), F32)], 1).T
        pieces.append(
            [jnp.broadcast_to(rates[h : h + 1], (SUBLANES, rows)) for h in range(lay.heads)]
        )
    return [
        cat([select_heads(lay, p, head_ids, shift) for p in pieces], 0)
        for shift in range(lay.heads)
    ]


def join_rows(lay, slabs):
    dim = lay.head_dim
    kind = BF16 if lay.packed else F32
    first = cat([s[:dim] for s in slabs], 1).astype(kind)
    second = cat([s[dim : 2 * dim] for s in slabs], 1).astype(kind)
    return first, second


def join_rates(lay, slabs):
    dim = lay.head_dim
    return cat([s[2 * dim : 2 * dim + 1] for s in slabs], 1)


def update_fn(lay, *args):
    slabs, weights = args[:-1], args[-1]
    keys, values = join_rows(lay, slabs)
    rates = join_rates(lay, slabs)
    gate, up, down = (split(lay, weights[m]) for m in range(3))
    a = dot_left(gate, keys, NN)
    b = dot_left(up, keys, NN)
    u = dot_left(down, values, NN)
    _, silu, _, slope = gates(a)
    mu = -rates * u
    d_gate = dot_left(split(lay, mu * b * slope), keys, NT)
    d_up = dot_left(split(lay, mu * silu), keys, NT)
    d_down = dot_left(split(lay, -rates * (silu * b)), values, NT)
    total = jnp.sum(rates, 1, keepdims=True)
    return pack_all(lay, (d_gate, d_up, d_down), total)


def norms(initial, moved):
    norm = jnp.sqrt(jnp.sum(initial * initial, 1, keepdims=True) + epsilon)
    inverse = lax.rsqrt(jnp.sum(moved * moved, 1, keepdims=True) + epsilon)
    return norm, inverse


def own_weights(lay, weights):
    return cat([weights[m][: lay.slot] for m in range(3)], 0)


def renorm_fn(lay, coefficient, *args):
    payloads, initial = args[:-1], args[-1]
    body, total = unpack(lay, functools.reduce(jnp.add, payloads))
    grad = body * (coefficient / total)
    moved = initial - grad
    norm, inverse = norms(initial, moved)
    return [pack(lay, moved * (norm * inverse), total), grad, moved]


def apply_fn(lay, *args):
    count = lay.plane
    payloads, slabs = args[:count], args[count:]
    queries, cotangents = join_rows(lay, slabs)
    weights = unpack_all(lay, payloads)
    gate, up, down = (split(lay, w) for w in weights)
    a = dot_left(gate, queries, NN)
    b = dot_left(up, queries, NN)
    u = dot_left(down, cotangents, NN)
    _, silu, _, slope = gates(a)
    da = split(lay, u * b * slope)
    db = split(lay, u * silu)
    h = split(lay, silu * b)
    d_gate = dot_left(da, queries, NT)
    d_up = dot_left(db, queries, NT)
    d_down = dot_left(h, cotangents, NT)
    outs = pack_all(lay, (d_gate, d_up, d_down), jnp.zeros((1, 1), F32))
    turned = split(lay, cat([weights[0], weights[1]], 0).T)
    both = tuple(cat([x, y], 0) for x, y in zip(da, db))
    d_query = dot_both(turned, both, NN)
    rows = slabs[0].shape[1]
    cut = [d_query[:, i * rows : (i + 1) * rows] for i in range(len(slabs))]
    heads = lay.heads
    return outs + [stack(cut[:heads])] + ([stack(cut[heads:])] if lay.cores > 1 else [])


def stack(parts):
    return cat([p[None] for p in parts], 0)


def renorm_back_fn(lay, coefficient, *args):
    payloads = args[: lay.plane]
    total_payload, initial, grad, moved = args[lay.plane :]
    d_new, _ = unpack(lay, functools.reduce(jnp.add, payloads))
    _, total = unpack(lay, total_payload)
    norm, inverse = norms(initial, moved)
    dots = jnp.sum(d_new * moved, 1, keepdims=True)
    d_moved = d_new * (norm * inverse) - moved * (dots * norm * inverse * inverse * inverse)
    direct = d_moved + initial * (dots * inverse / norm)
    d_update = -d_moved
    part = jnp.sum(jnp.sum(d_update * grad, 1, keepdims=True), 0, keepdims=True)
    return [pack(lay, d_update * (coefficient / total), -part / total), direct]


def pull_fn(lay, *args):
    count = lay.plane
    payloads, slabs, weights = args[:count], args[count:-1], args[-1]
    keys, values = join_rows(lay, slabs)
    rates = join_rates(lay, slabs)
    moves = unpack_all(lay, payloads)
    d_totals = functools.reduce(jnp.add, [unpack(lay, p)[1] for p in payloads])
    gate, up, down = (split(lay, weights[m]) for m in range(3))
    gate_move, up_move, down_move = (split(lay, w) for w in moves)
    a = dot_left(gate, keys, NN)
    b = dot_left(up, keys, NN)
    u = dot_left(down, values, NN)
    ta = dot_left(gate_move, keys, NN)
    tb = dot_left(up_move, keys, NN)
    w = dot_left(down_move, values, NN)
    sig, silu, rest, slope = gates(a)
    bend = sig * rest * (2.0 + a * (rest - sig))
    hidden = silu * b
    hidden_dot = slope * ta * b + silu * tb
    rate_part = -jnp.sum(w * hidden + u * hidden_dot, 0, keepdims=True)
    mu = -rates
    wm, um = mu * w, mu * u
    ga = split(lay, wm * b * slope + um * (bend * ta * b + slope * tb))
    gb = split(lay, wm * silu + um * slope * ta)
    gta = split(lay, um * slope * b)
    gtb = split(lay, um * silu)
    mh = split(lay, mu * hidden)
    md = split(lay, mu * hidden_dot)
    d_gate = dot_left(ga, keys, NT)
    d_up = dot_left(gb, keys, NT)
    d_down = dot_left(md, values, NT)
    outs = pack_all(lay, (d_gate, d_up, d_down), jnp.zeros((1, 1), F32))
    turned = split(lay, cat([weights[0], weights[1], moves[0], moves[1]], 0).T)
    stacked = tuple(cat(x, 0) for x in zip(ga, gb, gta, gtb))
    d_key = dot_both(turned, stacked, NN)
    turned = split(lay, cat([moves[2], weights[2]], 0).T)
    d_value = dot_both(turned, tuple(cat(x, 0) for x in zip(mh, md)), NN)
    rate_part = rate_part + d_totals
    rows = slabs[0].shape[1]
    cut = []
    for i in range(len(slabs)):
        take = slice(i * rows, (i + 1) * rows)
        rate_rows = jnp.broadcast_to(rate_part[:, take], (SUBLANES, rows))
        cut.append(cat([d_key[:, take], d_value[:, take], rate_rows], 0))
    heads = lay.heads
    return outs + [stack(cut[:heads])] + ([stack(cut[heads:])] if lay.cores > 1 else [])


def finish_fn(lay, count, *args):
    slabs, head_ids = args[:-1], args[-1]
    dim = lay.head_dim
    outs = []
    for n in range(count):
        pieces = [s[n * dim : (n + 1) * dim] for s in slabs]
        ordered = [
            select_heads(lay, pieces, lay.heads - head_ids, h) for h in range(lay.heads)
        ]
        outs.append(cat(ordered, 0).T.astype(BF16))
    if slabs[0].shape[0] > count * dim:
        pieces = [s[count * dim : count * dim + 1] for s in slabs]
        rows = [select_heads(lay, pieces, lay.heads - head_ids, h) for h in range(lay.heads)]
        rows.append(jnp.zeros((LANES - lay.heads, slabs[0].shape[1]), F32))
        outs.append(cat(rows, 0).T[:, : lay.heads])
    return outs


def run(lay, name, fn, args, always=False):
    if not (lay.packed or always):
        return fn(*args)
    shapes = jax.eval_shape(fn, *args)

    def kernel(*refs):
        ins, outs = refs[: len(args)], refs[len(args) :]
        for ref, value in zip(outs, fn(*[r[...] for r in ins])):
            ref[...] = value

    vmem = pl.BlockSpec(memory_space=pltpu.VMEM)
    return pl.pallas_call(
        kernel,
        out_shape=[jax.ShapeDtypeStruct(s.shape, s.dtype) for s in shapes],
        in_specs=[vmem] * len(args),
        out_specs=[vmem] * len(shapes),
        compiler_params=pltpu.CompilerParams(vmem_limit_bytes=40 * 1024 * 1024),
        name=name,
    )(*args)


def on_device(lay, queries, key_rows, value_rows, step_rates, fast_init, out_grad):
    head_dim, columns = fast_init.shape
    heads, slot, plane = lay.heads, lay.slot, lay.plane
    coefficient = step_size * math.sqrt(queries.shape[0] * lay.devices)
    view, patch = lax.axis_index("view"), lax.axis_index("patch")
    core = lax.rem(view, lay.cores)
    head = patch // lay.sub
    member = view // lay.cores * lay.sub + lax.rem(patch, lay.sub)
    me = view * lay.patches + patch
    head_ids = jnp.full((SUBLANES, LANES), head, jnp.int32)

    def send(x, perm):
        return lax.ppermute(x, AXES, perm)

    def to_heads(slabs):
        mine = [slabs[0]] + [send(slabs[s], lay.head_perm(s)) for s in range(1, heads)]
        others = [send(x, lay.core_perm()) for x in mine] if lay.cores > 1 else []
        return mine + others

    def from_heads(parts):
        mine = parts[0]
        if lay.cores > 1:
            mine = mine + send(parts[1], lay.core_perm())
        return [mine[0]] + [send(mine[s], lay.head_perm(heads - s)) for s in range(1, heads)]

    def scatter(payloads):
        moved = [send(payloads[r], lay.scatter_perm(r)) for r in range(1, plane)]
        return [payloads[0]] + moved

    def gather(payload):
        return [payload] + [send(payload, lay.gather_perm(r)) for r in range(1, plane)]

    fn = functools.partial
    kv = to_heads(
        run(lay, "spread_kv", fn(spread_rows, lay, True), (key_rows, value_rows, step_rates, head_ids), True)
    )
    qg = to_heads(run(lay, "spread_qg", fn(spread_rows, lay, False), (queries, out_grad, head_ids), True))

    first = head * lay.hidden + core * lay.half
    order = jnp.stack([lay.target(member, r) for r in range(plane)])
    turned = []
    for m in range(3):
        part = lax.dynamic_slice_in_dim(fast_init, m * heads * lay.hidden + first, lay.half, 1)
        turned.append(part.T.reshape(plane, slot, head_dim)[order].reshape(lay.half, head_dim))
    weights = jnp.stack(turned)
    own = jnp.concatenate([t[:slot] for t in turned], 0)

    sums = scatter(run(lay, "update", fn(update_fn, lay), (*kv, weights)))
    payload, grad, moved = run(lay, "renorm", fn(renorm_fn, lay, coefficient), (*sums, own))
    applied = run(lay, "apply", fn(apply_fn, lay), (*gather(payload), *qg))
    sums, query_parts = scatter(applied[:plane]), applied[plane:]
    d_payload, direct = run(
        lay, "renorm_back", fn(renorm_back_fn, lay, coefficient), (*sums, payload, own, grad, moved)
    )
    pulled = run(lay, "pull", fn(pull_fn, lay), (*gather(d_payload), *kv, weights))
    sums, key_parts = scatter(pulled[:plane]), pulled[plane:]
    (query_grad,) = run(
        lay, "finish_query", fn(finish_fn, lay, 1), (*from_heads(query_parts), head_ids), True
    )
    key_grad, value_grad, rate_grad = run(
        lay, "finish_key", fn(finish_fn, lay, 2), (*from_heads(key_parts), head_ids), True
    )

    def total_fn(*args):
        body, _ = unpack(lay, functools.reduce(jnp.add, args[:-1]))
        return [(body + args[-1]) / math.sqrt(queries.shape[0] * lay.devices)]

    (final,) = run(lay, "total", total_fn, (*sums, direct))
    pieces = final.reshape(3, slot, head_dim)
    arrived, places = [], []
    for chosen in lay.owner_rounds():
        which = jnp.array([m for _, _, m, _ in chosen], jnp.int32)[me]
        perm = [(i, o) for i, o, _, _ in chosen]
        spots = [0] * lay.devices
        for _, o, _, spot in chosen:
            spots[o] = spot
        arrived.append(send(lax.dynamic_index_in_dim(pieces, which, 0, False), perm))
        places.append(spots)
    rounds = [[places[t][i] for t in range(3)] for i in range(lay.devices)]
    inverse = jnp.array([[r.index(q) for q in range(3)] for r in rounds], jnp.int32)[me]
    fast_grad = jnp.stack(arrived)[inverse].reshape(3 * slot, head_dim).T
    return query_grad, key_grad, value_grad, rate_grad, fast_grad


def solution(mesh):
    rows = P(AXES, None)

    def whole(queries, key_rows, value_rows, step_rates, fast_init, out_grad):
        heads = step_rates.shape[1]
        head_dim, columns = fast_init.shape
        lay = Layout(
            mesh.shape["view"], mesh.shape["patch"], heads, columns // (3 * heads), head_dim
        )
        return jax.shard_map(
            functools.partial(on_device, lay),
            mesh=mesh,
            in_specs=(rows, rows, rows, rows, P(), rows),
            out_specs=(rows, rows, rows, rows, P(None, AXES)),
            check_vma=False,
        )(queries, key_rows, value_rows, step_rates, fast_init, out_grad)

    return whole
```

time: 493 us -> 144 us (0.29); the launches traced: 485 us -> 143 us
  waiting for transfers between devices: 325 us -> 50.2 us
  starting transfers between devices: 0.33 us -> 56.6 us
  local copies, waits for them, and re-layouts: 57.2 us -> 13 us
  blocking collectives: 42.4 us -> 0 us
  matrix products: 28.1 us -> 0 us
  other arithmetic: 17.3 us -> 3.17 us
  Pallas kernels: 0 us -> 13.7 us
  between operations: 15 us -> 6.77 us
    psum x2 -> x0, waiting for transfers between devices: 236 us -> none  [the longest x1 139 us: on_device(): d_new = lax.psum(flat_new, ('view', 'patch'))]
    unnamed x4 -> x0, waiting for transfers between devices: 88.4 us -> none
    ppermute x0 -> x40, starting transfers between devices: none -> 56.6 us  [send(): return lax.ppermute(x, AXES, perm)]
    ppermute x0 -> x40, waiting for transfers between devices: none -> 50.2 us  [send(): return lax.ppermute(x, AXES, perm)]
    psum x1 -> x0, blocking collectives: 42.4 us -> none  [rate_totals(): return lax.psum(jnp.sum(step_rates, 0), ('view', 'patch'))]
    dot_general x28 -> x0, matrix products: 28.1 us -> none  [the longest x9 9.98 us: fast_apply(): jnp.einsum('rhd,dhc->rhc', inputs, weights[:, 0], precision=product_preci...]
    reshape x6 -> x0, local copies, waits for them, and re-layouts: 21.3 us -> none  [the longest x1 5.42 us: on_device(): flat_new = new_part.reshape(head_dim, columns)]
    unnamed x131 -> x21, local copies, waits for them, and re-layouts: 23.4 us -> 6.23 us
  transfers between devices with their start and end apart: 3 -> 40, of which waited for: 3 -> 18; matrix products, arithmetic and copies ran while one was open for 3% -> 7% of each run, Pallas kernels for 0% -> 2%
where the time goes in v1:
time: 144 us; the launch traced here: 143 us
  starting transfers between devices  56.6 us (39%)
  waiting for transfers between devices  50.2 us (35%)
  Pallas kernels  13.7 us (10%)
  local copies, waits for them, and re-layouts  13 us (9%)
  between operations  6.77 us (5%)
  other arithmetic  3.17 us (2%)
    ppermute x40, starting transfers between devices, send(): return lax.ppermute(x, AXES, perm)  56.6 us
    ppermute x40, waiting for transfers between devices, send(): return lax.ppermute(x, AXES, perm)  50.2 us
    pallas_call x10, Pallas kernels, run(): pl.pallas_call(kernel, out_shape=[jax.ShapeDtypeStruct(s.shape, s.dtype)...  13.7 us
    unnamed x21, local copies, waits for them, and re-layouts  6.23 us
  transfers between devices with their start and end apart: 40, of which 18 were waited for; matrix products, arithmetic and copies ran while one was open for 7% of the time, Pallas kernels for 2%

profile of v1, /device:TPU:0, one launch (start us, length us, event | category | flops | bytes accessed | tf_op | source)
XLA Modules:
  0.0 143.4 jit_solution(6672640321903008470)
XLA Ops:
  1.5 0.9 copy-done
  2.4 0.9 copy-done.1
  3.5 3.1 %collective-permute-start = (f32[392,128]{1,0:T(8,128)S(1)}, f32[392,128]{1,0:T(8,128)S(1)}, u32[]{:S(2)}, u32[]{:S(2)}) collective-permute-start(f32[392,128]{1,0:T(8,128)S(1)} %get-tuple-element.38), channel_id=1, source_target_pairs={{0,2},{1,3},{2,4},{3,5},{4,6},{5,7},{6,0},{7,1},{8,10},{9,11},{10,... | collective-permute-start | bytes 602120 | tf_op jit(solution)/shard_map/ppermute | solution.py:385
  6.6 2.6 %collective-permute-start.1 = (f32[392,128]{1,0:T(8,128)S(1)}, f32[392,128]{1,0:T(8,128)S(1)}, u32[]{:S(2)}, u32[]{:S(2)}) collective-permute-start(f32[392,128]{1,0:T(8,128)S(1)} %get-tuple-element.39), channel_id=1, source_target_pairs={{0,4},{1,5},{2,6},{3,7},{4,0},{5,1},{6,2},{7,3},{8,12},{9,13},{10,... | collective-permute-start | bytes 602120 | tf_op jit(solution)/shard_map/ppermute | solution.py:385
  9.2 1.3 collective-permute-start.2
  10.6 0.9 copy-done.2
  11.5 0.9 copy-done.3
  13.4 1.4 constant_dynamic-slice_fusion.3
  16.9 9.7 %collective-permute-done.13.refs_5_ = f32[384,128]{1,0:T(8,128)S(1)} collective-permute-done((f32[384,128]{1,0:T(8,128)S(1)}, f32[384,128]{1,0:T(8,128)S(1)}, u32[]{:S(2)}, u32[]{:S(2)}) %collective-permute-start.13) | collective-permute-done | bytes 196640 | tf_op jit(solution)/shard_map/ppermute | solution.py:385
  26.6 5.5 %collective-permute-start.14 = (f32[384,128]{1,0:T(8,128)S(1)}, f32[384,128]{1,0:T(8,128)S(1)}, u32[]{:S(2)}, u32[]{:S(2)}) collective-permute-start(f32[384,128]{1,0:T(8,128)S(1)} %get-tuple-element.48), channel_id=1, source_target_pairs={{0,4},{1,5},{2,6},{3,7},{4,0},{5,1},{6,2},{7,3},{8,12},{9,13},{10,... | collective-permute-start | bytes 589832 | tf_op jit(solution)/shard_map/ppermute | solution.py:385
  34.2 1.9 %update.1 = (f32[224,128]{1,0:T(8,128)S(1)}, f32[224,128]{1,0:T(8,128)S(1)}, f32[224,128]{1,0:T(8,128)S(1)}, f32[224,128]{1,0:T(8,128)S(1)}) custom-call(f32[392,128]{1,0:T(8,128)S(1)} %get-tuple-element.37.refs_0_.refs_4_, f32[392,128]{1,0:T(8,128)S(1)} %collective-permute-done.refs_1_.refs_5_, f32[392,128]{1,0:T(8,128)S(1)} %collective-permute-done.1.refs_2_.refs_6_, ...), custom_call_target="tpu_custom_call" | custom-call | tf_op jit(solution)/shard_map/update/pallas_call | solution.py:363
  36.1 1.6 %collective-permute-start.7 = (f32[224,128]{1,0:T(8,128)S(1)}, f32[224,128]{1,0:T(8,128)S(1)}, u32[]{:S(2)}, u32[]{:S(2)}) collective-permute-start(f32[224,128]{1,0:T(8,128)S(1)} %get-tuple-element.42), channel_id=1, source_target_pairs={{0,1},{1,0},{2,3},{3,2},{4,5},{5,4},{6,7},{7,6},{8,9},{9,8},{10,11... | collective-permute-start | bytes 344072 | tf_op jit(solution)/shard_map/ppermute | solution.py:385
  37.7 2.4 %collective-permute-done.14.refs_6_ = f32[384,128]{1,0:T(8,128)S(1)} collective-permute-done((f32[384,128]{1,0:T(8,128)S(1)}, f32[384,128]{1,0:T(8,128)S(1)}, u32[]{:S(2)}, u32[]{:S(2)}) %collective-permute-start.14) | collective-permute-done | bytes 196640 | tf_op jit(solution)/shard_map/ppermute | solution.py:385
  40.1 1.5 %collective-permute-start.8 = (f32[224,128]{1,0:T(8,128)S(1)}, f32[224,128]{1,0:T(8,128)S(1)}, u32[]{:S(2)}, u32[]{:S(2)}) collective-permute-start(f32[224,128]{1,0:T(8,128)S(1)} %get-tuple-element.43), channel_id=1, source_target_pairs={{0,16},{1,17},{2,18},{3,19},{4,20},{5,21},{6,22},{7,23},{8,24},{9,... | collective-permute-start | bytes 344072 | tf_op jit(solution)/shard_map/ppermute | solution.py:385
  41.6 1.7 %collective-permute-done.15.refs_7_ = f32[384,128]{1,0:T(8,128)S(1)} collective-permute-done((f32[384,128]{1,0:T(8,128)S(1)}, f32[384,128]{1,0:T(8,128)S(1)}, u32[]{:S(2)}, u32[]{:S(2)}) %collective-permute-start.15) | collective-permute-done | bytes 196640 | tf_op jit(solution)/shard_map/ppermute | solution.py:385
  43.8 1.0 collective-permute-done.8.refs_2_
  44.9 2.4 %collective-permute-start.9 = (f32[224,128]{1,0:T(8,128)S(1)}, f32[224,128]{1,0:T(8,128)S(1)}, u32[]{:S(2)}, u32[]{:S(2)}) collective-permute-start(f32[224,128]{1,0:T(8,128)S(1)} %get-tuple-element.44), channel_id=1, source_target_pairs={{0,17},{1,16},{2,19},{3,18},{4,21},{5,20},{6,23},{7,22},{8,25},{9,... | collective-permute-start | bytes 344072 | tf_op jit(solution)/shard_map/ppermute | solution.py:385
  47.3 3.2 %collective-permute-done.9.refs_3_ = f32[224,128]{1,0:T(8,128)S(1)} collective-permute-done((f32[224,128]{1,0:T(8,128)S(1)}, f32[224,128]{1,0:T(8,128)S(1)}, u32[]{:S(2)}, u32[]{:S(2)}) %collective-permute-start.9) | collective-permute-done | bytes 114720 | tf_op jit(solution)/shard_map/ppermute | solution.py:385
  50.8 1.6 %collective-permute-start.10 = (f32[224,128]{1,0:T(8,128)S(1)}, f32[224,128]{1,0:T(8,128)S(1)}, u32[]{:S(2)}, u32[]{:S(2)}) collective-permute-start(f32[224,128]{1,0:T(8,128)S(1)} %get-tuple-element.45.refs_0_.refs_4_), channel_id=1, source_target_pairs={{0,1},{1,0},{2,3},{3,2},{4,5},{5,4},{6,7},{7,6},{8,9},{9,8},{10,11... | collective-permute-start | bytes 344072 | tf_op jit(solution)/shard_map/ppermute | solution.py:385
  52.4 1.5 %collective-permute-start.11 = (f32[224,128]{1,0:T(8,128)S(1)}, f32[224,128]{1,0:T(8,128)S(1)}, u32[]{:S(2)}, u32[]{:S(2)}) collective-permute-start(f32[224,128]{1,0:T(8,128)S(1)} %get-tuple-element.45.refs_0_.refs_4_), channel_id=1, source_target_pairs={{0,16},{1,17},{2,18},{3,19},{4,20},{5,21},{6,22},{7,23},{8,24},{9,... | collective-permute-start | bytes 344072 | tf_op jit(solution)/shard_map/ppermute | solution.py:385
  54.4 2.5 %collective-permute-done.10.refs_1_ = f32[224,128]{1,0:T(8,128)S(1)} collective-permute-done((f32[224,128]{1,0:T(8,128)S(1)}, f32[224,128]{1,0:T(8,128)S(1)}, u32[]{:S(2)}, u32[]{:S(2)}) %collective-permute-start.10) | collective-permute-done | bytes 114720 | tf_op jit(solution)/shard_map/ppermute | solution.py:385
  57.2 2.4 %collective-permute-done.12.refs_3_ = f32[224,128]{1,0:T(8,128)S(1)} collective-permute-done((f32[224,128]{1,0:T(8,128)S(1)}, f32[224,128]{1,0:T(8,128)S(1)}, u32[]{:S(2)}, u32[]{:S(2)}) %collective-permute-start.12) | collective-permute-done | bytes 114720 | tf_op jit(solution)/shard_map/ppermute | solution.py:385
  59.6 3.6 %apply.1 = (f32[224,128]{1,0:T(8,128)S(1)}, f32[224,128]{1,0:T(8,128)S(1)}, f32[224,128]{1,0:T(8,128)S(1)}, f32[224,128]{1,0:T(8,128)S(1)}, f32[4,192,128]{2,1,0:T(8,128)S(1)}, /*index=5*/f32[4,192,128]{2,1,0:T(8,128)}) custom-call(f32[224,128]{1,0:T(8,128)S(1)} %get-tuple-element.45.refs_0_.refs_4_, f32[224,128]{1,0:T(8,128)S(1)} %collective-permute-done.10.refs_1_, ...), custom_call_target="tpu_custom_call" | custom-call | tf_op jit(solution)/shard_map/apply/pallas_call | solution.py:363
  63.7 1.3 collective-permute-start.25
  65.0 1.7 %collective-permute-start.26 = (f32[224,128]{1,0:T(8,128)S(1)}, f32[224,128]{1,0:T(8,128)S(1)}, u32[]{:S(2)}, u32[]{:S(2)}) collective-permute-start(f32[224,128]{1,0:T(8,128)S(1)} %get-tuple-element.55), channel_id=1, source_target_pairs={{0,17},{1,16},{2,19},{3,18},{4,21},{5,20},{6,23},{7,22},{8,25},{9,... | collective-permute-start | bytes 344072 | tf_op jit(solution)/shard_map/ppermute | solution.py:385
  66.7 1.3 collective-permute-done.24.refs_1_
  68.5 3.1 %collective-permute-done.26.refs_3_ = f32[224,128]{1,0:T(8,128)S(1)} collective-permute-done((f32[224,128]{1,0:T(8,128)S(1)}, f32[224,128]{1,0:T(8,128)S(1)}, u32[]{:S(2)}, u32[]{:S(2)}) %collective-permute-start.26) | collective-permute-done | bytes 114720 | tf_op jit(solution)/shard_map/ppermute | solution.py:385
  72.0 1.1 collective-permute-start.27
  73.1 1.5 %collective-permute-start.28 = (f32[224,128]{1,0:T(8,128)S(1)}, f32[224,128]{1,0:T(8,128)S(1)}, u32[]{:S(2)}, u32[]{:S(2)}) collective-permute-start(f32[224,128]{1,0:T(8,128)S(1)} %get-tuple-element.58.refs_0_), channel_id=1, source_target_pairs={{0,16},{1,17},{2,18},{3,19},{4,20},{5,21},{6,22},{7,23},{8,24},{9,... | collective-permute-start | bytes 344072 | tf_op jit(solution)/shard_map/ppermute | solution.py:385
  74.6 1.0 collective-permute-start.29
  75.5 1.3 collective-permute-done.27.refs_1_
  76.9 1.0 collective-permute-done.28.refs_2_
  77.9 2.4 %collective-permute-done.29.refs_3_ = f32[224,128]{1,0:T(8,128)S(1)} collective-permute-done((f32[224,128]{1,0:T(8,128)S(1)}, f32[224,128]{1,0:T(8,128)S(1)}, u32[]{:S(2)}, u32[]{:S(2)}) %collective-permute-start.29) | collective-permute-done | bytes 114720 | tf_op jit(solution)/shard_map/ppermute | solution.py:385
  80.3 5.3 %pull.1 = (f32[224,128]{1,0:T(8,128)S(1)}, f32[224,128]{1,0:T(8,128)}, f32[224,128]{1,0:T(8,128)S(1)}, f32[224,128]{1,0:T(8,128)S(1)}, f32[4,392,128]{2,1,0:T(8,128)S(1)}, /*index=5*/f32[4,392,128]{2,1,0:T(8,128)S(1)}) custom-call(f32[224,128]{1,0:T(8,128)S(1)} %get-tuple-element.58.refs_0_, f32[224,128]{1,0:T(8,128)S(1)} %collective-permute-done.27.refs_1_, ...), custom_call_target="tpu_custom_call" | custom-call | tf_op jit(solution)/shard_map/pull/pallas_call | solution.py:363
  86.6 1.3 collective-permute-start.35
  87.9 1.7 %collective-permute-start.36 = (f32[224,128]{1,0:T(8,128)S(1)}, f32[224,128]{1,0:T(8,128)S(1)}, u32[]{:S(2)}, u32[]{:S(2)}) collective-permute-start(f32[224,128]{1,0:T(8,128)S(1)} %get-tuple-element.67), channel_id=1, source_target_pairs={{0,17},{1,16},{2,19},{3,18},{4,21},{5,20},{6,23},{7,22},{8,25},{9,... | collective-permute-start | bytes 344072 | tf_op jit(solution)/shard_map/ppermute | solution.py:385
  98.7 7.4 %collective-permute-start.38 = (f32[48,192]{1,0:T(8,128)S(1)}, f32[48,192]{1,0:T(8,128)S(1)}, u32[]{:S(2)}, u32[]{:S(2)}) collective-permute-start(f32[48,192]{1,0:T(8,128)S(1)} %get-tuple-element.92), channel_id=1, source_target_pairs={{0,10},{1,0},{2,24},{3,13},{4,26},{5,16},{6,29},{7,19},{8,1},{9,23... | collective-permute-start | bytes 110600 | tf_op jit(solution)/shard_map/ppermute | solution.py:385
  106.1 5.2 %collective-permute-start.39 = (f32[48,192]{1,0:T(8,128)S(1)}, f32[48,192]{1,0:T(8,128)S(1)}, u32[]{:S(2)}, u32[]{:S(2)}) collective-permute-start(f32[48,192]{1,0:T(8,128)S(1)} %get-tuple-element.91), channel_id=1, source_target_pairs={{0,21},{1,11},{2,2},{3,24},{4,16},{5,5},{6,8},{7,29},{8,12},{9,1},... | collective-permute-start | bytes 110600 | tf_op jit(solution)/shard_map/ppermute | solution.py:385
  112.1 1.1 add.74
  114.5 1.3 add.75
  115.8 0.9 collective-permute-start.31
  116.7 2.0 %collective-permute-start.32 = (f32[392,128]{1,0:T(8,128)S(1)}, f32[392,128]{1,0:T(8,128)S(1)}, u32[]{:S(2)}, u32[]{:S(2)}) collective-permute-start(f32[392,128]{1,0:T(8,128)S(1)} %get-tuple-element.83), channel_id=1, source_target_pairs={{0,4},{1,5},{2,6},{3,7},{4,0},{5,1},{6,2},{7,3},{8,12},{9,13},{10,... | collective-permute-start | bytes 602120 | tf_op jit(solution)/shard_map/ppermute | solution.py:385
  118.7 2.1 %collective-permute-start.22 = (f32[192,128]{1,0:T(8,128)}, f32[192,128]{1,0:T(8,128)S(1)}, u32[]{:S(2)}, u32[]{:S(2)}) collective-permute-start(f32[192,128]{1,0:T(8,128)} %get-tuple-element.87), channel_id=1, source_target_pairs={{0,4},{1,5},{2,6},{3,7},{4,0},{5,1},{6,2},{7,3},{8,12},{9,13},{10,... | collective-permute-start | bytes 294920 | tf_op jit(solution)/shard_map/ppermute | solution.py:385
  120.9 2.3 %collective-permute-start.23 = (f32[192,128]{1,0:T(8,128)S(1)}, f32[192,128]{1,0:T(8,128)S(1)}, u32[]{:S(2)}, u32[]{:S(2)}) collective-permute-start(f32[192,128]{1,0:T(8,128)S(1)} %get-tuple-element.86), channel_id=1, source_target_pairs={{0,2},{1,3},{2,4},{3,5},{4,6},{5,7},{6,0},{7,1},{8,10},{9,11},{10,... | collective-permute-start | bytes 294920 | tf_op jit(solution)/shard_map/ppermute | solution.py:385
  123.2 1.2 gather_fusion.3
  124.4 16.6 %collective-permute-done.22.refs_2_ = f32[192,128]{1,0:T(8,128)S(1)} collective-permute-done((f32[192,128]{1,0:T(8,128)}, f32[192,128]{1,0:T(8,128)S(1)}, u32[]{:S(2)}, u32[]{:S(2)}) %collective-permute-start.22) | collective-permute-done | bytes 98336 | tf_op jit(solution)/shard_map/ppermute | solution.py:385
  141.0 0.8 finish_query.1
  141.8 0.9 finish_key.1
  (86 shorter events, 16.1 us)
Async XLA Ops:
  1.4 0.9 copy-start
  2.4 0.9 copy-start.1
  3.5 28.6 %collective-permute-start = (f32[392,128]{1,0:T(8,128)S(1)}, f32[392,128]{1,0:T(8,128)S(1)}, u32[]{:S(2)}, u32[]{:S(2)}) collective-permute-start(f32[392,128]{1,0:T(8,128)S(1)} %get-tuple-element.38), channel_id=1, source_target_pairs={{0,2},{1,3},{2,4},{3,5},{4,6},{5,7},{6,0},{7,1},{8,10},{9,11},{10,... | collective-permute-start | bytes 602120 | tf_op jit(solution)/shard_map/ppermute | solution.py:385
  6.6 25.5 %collective-permute-start.1 = (f32[392,128]{1,0:T(8,128)S(1)}, f32[392,128]{1,0:T(8,128)S(1)}, u32[]{:S(2)}, u32[]{:S(2)}) collective-permute-start(f32[392,128]{1,0:T(8,128)S(1)} %get-tuple-element.39), channel_id=1, source_target_pairs={{0,4},{1,5},{2,6},{3,7},{4,0},{5,1},{6,2},{7,3},{8,12},{9,13},{10,... | collective-permute-start | bytes 602120 | tf_op jit(solution)/shard_map/ppermute | solution.py:385
  9.2 23.5 %collective-permute-start.2 = (f32[392,128]{1,0:T(8,128)S(1)}, f32[392,128]{1,0:T(8,128)S(1)}, u32[]{:S(2)}, u32[]{:S(2)}) collective-permute-start(f32[392,128]{1,0:T(8,128)S(1)} %get-tuple-element.40), channel_id=1, source_target_pairs={{0,6},{1,7},{2,0},{3,1},{4,2},{5,3},{6,4},{7,5},{8,14},{9,15},{10,... | collective-permute-start | bytes 602120 | tf_op jit(solution)/shard_map/ppermute | solution.py:385
  10.6 22.2 %collective-permute-start.3 = (f32[392,128]{1,0:T(8,128)S(1)}, f32[392,128]{1,0:T(8,128)S(1)}, u32[]{:S(2)}, u32[]{:S(2)}) collective-permute-start(f32[392,128]{1,0:T(8,128)S(1)} %get-tuple-element.37.refs_0_.refs_4_), channel_id=1, source_target_pairs={{0,8},{1,9},{2,10},{3,11},{4,12},{5,13},{6,14},{7,15},{8,0},{9,1},... | collective-permute-start | bytes 602120 | tf_op jit(solution)/shard_map/ppermute | solution.py:385
  10.6 0.9 copy-start.2
  11.5 0.9 copy-start.3
  12.6 14.0 %collective-permute-start.13 = (f32[384,128]{1,0:T(8,128)S(1)}, f32[384,128]{1,0:T(8,128)S(1)}, u32[]{:S(2)}, u32[]{:S(2)}) collective-permute-start(f32[384,128]{1,0:T(8,128)S(1)} %get-tuple-element.47), channel_id=1, source_target_pairs={{0,2},{1,3},{2,4},{3,5},{4,6},{5,7},{6,0},{7,1},{8,10},{9,11},{10,... | collective-permute-start | bytes 589832 | tf_op jit(solution)/shard_map/ppermute | solution.py:385
  26.6 13.5 %collective-permute-start.14 = (f32[384,128]{1,0:T(8,128)S(1)}, f32[384,128]{1,0:T(8,128)S(1)}, u32[]{:S(2)}, u32[]{:S(2)}) collective-permute-start(f32[384,128]{1,0:T(8,128)S(1)} %get-tuple-element.48), channel_id=1, source_target_pairs={{0,4},{1,5},{2,6},{3,7},{4,0},{5,1},{6,2},{7,3},{8,12},{9,13},{10,... | collective-permute-start | bytes 589832 | tf_op jit(solution)/shard_map/ppermute | solution.py:385
  32.1 1.4 %collective-permute-start.4 = (f32[392,128]{1,0:T(8,128)S(1)}, f32[392,128]{1,0:T(8,128)S(1)}, u32[]{:S(2)}, u32[]{:S(2)}) collective-permute-start(f32[392,128]{1,0:T(8,128)S(1)} %collective-permute-done.refs_1_.refs_5_), channel_id=1, source_target_pairs={{0,8},{1,9},{2,10},{3,11},{4,12},{5,13},{6,14},{7,15},{8,0},{9,1},... | collective-permute-start | bytes 602120 | tf_op jit(solution)/shard_map/ppermute | solution.py:385
  32.2 1.7 %collective-permute-start.5 = (f32[392,128]{1,0:T(8,128)S(1)}, f32[392,128]{1,0:T(8,128)S(1)}, u32[]{:S(2)}, u32[]{:S(2)}) collective-permute-start(f32[392,128]{1,0:T(8,128)S(1)} %collective-permute-done.1.refs_2_.refs_6_), channel_id=1, source_target_pairs={{0,8},{1,9},{2,10},{3,11},{4,12},{5,13},{6,14},{7,15},{8,0},{9,1},... | collective-permute-start | bytes 602120 | tf_op jit(solution)/shard_map/ppermute | solution.py:385
  32.7 1.5 %collective-permute-start.6 = (f32[392,128]{1,0:T(8,128)S(1)}, f32[392,128]{1,0:T(8,128)S(1)}, u32[]{:S(2)}, u32[]{:S(2)}) collective-permute-start(f32[392,128]{1,0:T(8,128)S(1)} %collective-permute-done.2.refs_3_.refs_7_), channel_id=1, source_target_pairs={{0,8},{1,9},{2,10},{3,11},{4,12},{5,13},{6,14},{7,15},{8,0},{9,1},... | collective-permute-start | bytes 602120 | tf_op jit(solution)/shard_map/ppermute | solution.py:385
  32.8 10.6 %collective-permute-start.15 = (f32[384,128]{1,0:T(8,128)S(1)}, f32[384,128]{1,0:T(8,128)S(1)}, u32[]{:S(2)}, u32[]{:S(2)}) collective-permute-start(f32[384,128]{1,0:T(8,128)S(1)} %get-tuple-element.49), channel_id=1, source_target_pairs={{0,6},{1,7},{2,0},{3,1},{4,2},{5,3},{6,4},{7,5},{8,14},{9,15},{10,... | collective-permute-start | bytes 589832 | tf_op jit(solution)/shard_map/ppermute | solution.py:385
  33.6 18.8 %collective-permute-start.16 = (f32[384,128]{1,0:T(8,128)S(1)}, f32[384,128]{1,0:T(8,128)S(1)}, u32[]{:S(2)}, u32[]{:S(2)}) collective-permute-start(f32[384,128]{1,0:T(8,128)S(1)} %get-tuple-element.46.refs_4_), channel_id=1, source_target_pairs={{0,8},{1,9},{2,10},{3,11},{4,12},{5,13},{6,14},{7,15},{8,0},{9,1},... | collective-permute-start | bytes 589832 | tf_op jit(solution)/shard_map/ppermute | solution.py:385
  33.9 20.0 %collective-permute-start.17 = (f32[384,128]{1,0:T(8,128)S(1)}, f32[384,128]{1,0:T(8,128)S(1)}, u32[]{:S(2)}, u32[]{:S(2)}) collective-permute-start(f32[384,128]{1,0:T(8,128)S(1)} %collective-permute-done.13.refs_5_), channel_id=1, source_target_pairs={{0,8},{1,9},{2,10},{3,11},{4,12},{5,13},{6,14},{7,15},{8,0},{9,1},... | collective-permute-start | bytes 589832 | tf_op jit(solution)/shard_map/ppermute | solution.py:385
  36.1 53.5 %copy-start.7 = (s32[32]{0:T(128)S(1)}, s32[32]{0:T(128)}, u32[]{:S(2)}) copy-start(s32[32]{0:T(128)} %constant.73.clone) | copy-start | bytes 388
  36.1 55.4 %copy-start.6 = (s32[32]{0:T(128)S(1)}, s32[32]{0:T(128)}, u32[]{:S(2)}) copy-start(s32[32]{0:T(128)} %constant.74.clone) | copy-start | bytes 388
  36.1 57.2 %copy-start.5 = (s32[32]{0:T(128)S(1)}, s32[32]{0:T(128)}, u32[]{:S(2)}) copy-start(s32[32]{0:T(128)} %constant.75.clone) | copy-start | bytes 388
  36.1 7.2 %collective-permute-start.7 = (f32[224,128]{1,0:T(8,128)S(1)}, f32[224,128]{1,0:T(8,128)S(1)}, u32[]{:S(2)}, u32[]{:S(2)}) collective-permute-start(f32[224,128]{1,0:T(8,128)S(1)} %get-tuple-element.42), channel_id=1, source_target_pairs={{0,1},{1,0},{2,3},{3,2},{4,5},{5,4},{6,7},{7,6},{8,9},{9,8},{10,11... | collective-permute-start | bytes 344072 | tf_op jit(solution)/shard_map/ppermute | solution.py:385
  40.1 4.8 %collective-permute-start.8 = (f32[224,128]{1,0:T(8,128)S(1)}, f32[224,128]{1,0:T(8,128)S(1)}, u32[]{:S(2)}, u32[]{:S(2)}) collective-permute-start(f32[224,128]{1,0:T(8,128)S(1)} %get-tuple-element.43), channel_id=1, source_target_pairs={{0,16},{1,17},{2,18},{3,19},{4,20},{5,21},{6,22},{7,23},{8,24},{9,... | collective-permute-start | bytes 344072 | tf_op jit(solution)/shard_map/ppermute | solution.py:385
  43.3 11.1 %collective-permute-start.18 = (f32[384,128]{1,0:T(8,128)S(1)}, f32[384,128]{1,0:T(8,128)S(1)}, u32[]{:S(2)}, u32[]{:S(2)}) collective-permute-start(f32[384,128]{1,0:T(8,128)S(1)} %collective-permute-done.14.refs_6_), channel_id=1, source_target_pairs={{0,8},{1,9},{2,10},{3,11},{4,12},{5,13},{6,14},{7,15},{8,0},{9,1},... | collective-permute-start | bytes 589832 | tf_op jit(solution)/shard_map/ppermute | solution.py:385
  43.3 11.1 %collective-permute-start.19 = (f32[384,128]{1,0:T(8,128)S(1)}, f32[384,128]{1,0:T(8,128)S(1)}, u32[]{:S(2)}, u32[]{:S(2)}) collective-permute-start(f32[384,128]{1,0:T(8,128)S(1)} %collective-permute-done.15.refs_7_), channel_id=1, source_target_pairs={{0,8},{1,9},{2,10},{3,11},{4,12},{5,13},{6,14},{7,15},{8,0},{9,1},... | collective-permute-start | bytes 589832 | tf_op jit(solution)/shard_map/ppermute | solution.py:385
  44.9 5.7 %collective-permute-start.9 = (f32[224,128]{1,0:T(8,128)S(1)}, f32[224,128]{1,0:T(8,128)S(1)}, u32[]{:S(2)}, u32[]{:S(2)}) collective-permute-start(f32[224,128]{1,0:T(8,128)S(1)} %get-tuple-element.44), channel_id=1, source_target_pairs={{0,17},{1,16},{2,19},{3,18},{4,21},{5,20},{6,23},{7,22},{8,25},{9,... | collective-permute-start | bytes 344072 | tf_op jit(solution)/shard_map/ppermute | solution.py:385
  50.8 6.1 %collective-permute-start.10 = (f32[224,128]{1,0:T(8,128)S(1)}, f32[224,128]{1,0:T(8,128)S(1)}, u32[]{:S(2)}, u32[]{:S(2)}) collective-permute-start(f32[224,128]{1,0:T(8,128)S(1)} %get-tuple-element.45.refs_0_.refs_4_), channel_id=1, source_target_pairs={{0,1},{1,0},{2,3},{3,2},{4,5},{5,4},{6,7},{7,6},{8,9},{9,8},{10,11... | collective-permute-start | bytes 344072 | tf_op jit(solution)/shard_map/ppermute | solution.py:385
  52.4 4.8 %collective-permute-start.11 = (f32[224,128]{1,0:T(8,128)S(1)}, f32[224,128]{1,0:T(8,128)S(1)}, u32[]{:S(2)}, u32[]{:S(2)}) collective-permute-start(f32[224,128]{1,0:T(8,128)S(1)} %get-tuple-element.45.refs_0_.refs_4_), channel_id=1, source_target_pairs={{0,16},{1,17},{2,18},{3,19},{4,20},{5,21},{6,22},{7,23},{8,24},{9,... | collective-permute-start | bytes 344072 | tf_op jit(solution)/shard_map/ppermute | solution.py:385
  53.9 5.7 %collective-permute-start.12 = (f32[224,128]{1,0:T(8,128)S(1)}, f32[224,128]{1,0:T(8,128)S(1)}, u32[]{:S(2)}, u32[]{:S(2)}) collective-permute-start(f32[224,128]{1,0:T(8,128)S(1)} %get-tuple-element.45.refs_0_.refs_4_), channel_id=1, source_target_pairs={{0,17},{1,16},{2,19},{3,18},{4,21},{5,20},{6,23},{7,22},{8,25},{9,... | collective-permute-start | bytes 344072 | tf_op jit(solution)/shard_map/ppermute | solution.py:385
  63.2 4.8 %collective-permute-start.24 = (f32[224,128]{1,0:T(8,128)S(1)}, f32[224,128]{1,0:T(8,128)S(1)}, u32[]{:S(2)}, u32[]{:S(2)}) collective-permute-start(f32[224,128]{1,0:T(8,128)S(1)} %get-tuple-element.53), channel_id=1, source_target_pairs={{0,1},{1,0},{2,3},{3,2},{4,5},{5,4},{6,7},{7,6},{8,9},{9,8},{10,11... | collective-permute-start | bytes 344072 | tf_op jit(solution)/shard_map/ppermute | solution.py:385
  63.7 4.8 %collective-permute-start.25 = (f32[224,128]{1,0:T(8,128)S(1)}, f32[224,128]{1,0:T(8,128)S(1)}, u32[]{:S(2)}, u32[]{:S(2)}) collective-permute-start(f32[224,128]{1,0:T(8,128)S(1)} %get-tuple-element.54), channel_id=1, source_target_pairs={{0,16},{1,17},{2,18},{3,19},{4,20},{5,21},{6,22},{7,23},{8,24},{9,... | collective-permute-start | bytes 344072 | tf_op jit(solution)/shard_map/ppermute | solution.py:385
  65.0 6.7 %collective-permute-start.26 = (f32[224,128]{1,0:T(8,128)S(1)}, f32[224,128]{1,0:T(8,128)S(1)}, u32[]{:S(2)}, u32[]{:S(2)}) collective-permute-start(f32[224,128]{1,0:T(8,128)S(1)} %get-tuple-element.55), channel_id=1, source_target_pairs={{0,17},{1,16},{2,19},{3,18},{4,21},{5,20},{6,23},{7,22},{8,25},{9,... | collective-permute-start | bytes 344072 | tf_op jit(solution)/shard_map/ppermute | solution.py:385
  72.0 4.9 %collective-permute-start.27 = (f32[224,128]{1,0:T(8,128)S(1)}, f32[224,128]{1,0:T(8,128)S(1)}, u32[]{:S(2)}, u32[]{:S(2)}) collective-permute-start(f32[224,128]{1,0:T(8,128)S(1)} %get-tuple-element.58.refs_0_), channel_id=1, source_target_pairs={{0,1},{1,0},{2,3},{3,2},{4,5},{5,4},{6,7},{7,6},{8,9},{9,8},{10,11... | collective-permute-start | bytes 344072 | tf_op jit(solution)/shard_map/ppermute | solution.py:385
  73.1 4.8 %collective-permute-start.28 = (f32[224,128]{1,0:T(8,128)S(1)}, f32[224,128]{1,0:T(8,128)S(1)}, u32[]{:S(2)}, u32[]{:S(2)}) collective-permute-start(f32[224,128]{1,0:T(8,128)S(1)} %get-tuple-element.58.refs_0_), channel_id=1, source_target_pairs={{0,16},{1,17},{2,18},{3,19},{4,20},{5,21},{6,22},{7,23},{8,24},{9,... | collective-permute-start | bytes 344072 | tf_op jit(solution)/shard_map/ppermute | solution.py:385
  74.6 5.7 %collective-permute-start.29 = (f32[224,128]{1,0:T(8,128)S(1)}, f32[224,128]{1,0:T(8,128)S(1)}, u32[]{:S(2)}, u32[]{:S(2)}) collective-permute-start(f32[224,128]{1,0:T(8,128)S(1)} %get-tuple-element.58.refs_0_), channel_id=1, source_target_pairs={{0,17},{1,16},{2,19},{3,18},{4,21},{5,20},{6,23},{7,22},{8,25},{9,... | collective-permute-start | bytes 344072 | tf_op jit(solution)/shard_map/ppermute | solution.py:385
  85.6 28.9 %collective-permute-start.30 = (f32[4,392,128]{2,1,0:T(8,128)S(1)}, f32[4,392,128]{2,1,0:T(8,128)}, u32[]{:S(2)}, u32[]{:S(2)}) collective-permute-start(f32[4,392,128]{2,1,0:T(8,128)S(1)} %get-tuple-element.60), channel_id=1, source_target_pairs={{0,8},{1,9},{2,10},{3,11},{4,12},{5,13},{6,14},{7,15},{8,0},{9,1},... | collective-permute-start | bytes 2408456 | tf_op jit(solution)/shard_map/ppermute | solution.py:385
  85.6 25.8 %collective-permute-start.20 = (f32[4,192,128]{2,1,0:T(8,128)}, f32[4,192,128]{2,1,0:T(8,128)S(1)}, u32[]{:S(2)}, u32[]{:S(2)}) collective-permute-start(f32[4,192,128]{2,1,0:T(8,128)} %get-tuple-element.51), channel_id=1, source_target_pairs={{0,8},{1,9},{2,10},{3,11},{4,12},{5,13},{6,14},{7,15},{8,0},{9,1},... | collective-permute-start | bytes 1179656 | tf_op jit(solution)/shard_map/ppermute | solution.py:385
  86.1 11.8 %collective-permute-start.34 = (f32[224,128]{1,0:T(8,128)}, f32[224,128]{1,0:T(8,128)S(1)}, u32[]{:S(2)}, u32[]{:S(2)}) collective-permute-start(f32[224,128]{1,0:T(8,128)} %get-tuple-element.65), channel_id=1, source_target_pairs={{0,1},{1,0},{2,3},{3,2},{4,5},{5,4},{6,7},{7,6},{8,9},{9,8},{10,11... | collective-permute-start | bytes 344072 | tf_op jit(solution)/shard_map/ppermute | solution.py:385
  86.6 11.3 %collective-permute-start.35 = (f32[224,128]{1,0:T(8,128)S(1)}, f32[224,128]{1,0:T(8,128)S(1)}, u32[]{:S(2)}, u32[]{:S(2)}) collective-permute-start(f32[224,128]{1,0:T(8,128)S(1)} %get-tuple-element.66), channel_id=1, source_target_pairs={{0,16},{1,17},{2,18},{3,19},{4,20},{5,21},{6,22},{7,23},{8,24},{9,... | collective-permute-start | bytes 344072 | tf_op jit(solution)/shard_map/ppermute | solution.py:385
  87.9 10.0 %collective-permute-start.36 = (f32[224,128]{1,0:T(8,128)S(1)}, f32[224,128]{1,0:T(8,128)S(1)}, u32[]{:S(2)}, u32[]{:S(2)}) collective-permute-start(f32[224,128]{1,0:T(8,128)S(1)} %get-tuple-element.67), channel_id=1, source_target_pairs={{0,17},{1,16},{2,19},{3,18},{4,21},{5,20},{6,23},{7,22},{8,25},{9,... | collective-permute-start | bytes 344072 | tf_op jit(solution)/shard_map/ppermute | solution.py:385
  98.0 18.6 %collective-permute-start.37 = (f32[48,192]{1,0:T(8,128)S(1)}, f32[48,192]{1,0:T(8,128)S(1)}, u32[]{:S(2)}, u32[]{:S(2)}) collective-permute-start(f32[48,192]{1,0:T(8,128)S(1)} %get-tuple-element.90), channel_id=1, source_target_pairs={{0,0},{1,21},{2,13},{3,3},{4,5},{5,27},{6,18},{7,8},{8,22},{9,12},... | collective-permute-start | bytes 110600 | tf_op jit(solution)/shard_map/ppermute | solution.py:385
  98.7 20.0 %collective-permute-start.38 = (f32[48,192]{1,0:T(8,128)S(1)}, f32[48,192]{1,0:T(8,128)S(1)}, u32[]{:S(2)}, u32[]{:S(2)}) collective-permute-start(f32[48,192]{1,0:T(8,128)S(1)} %get-tuple-element.92), channel_id=1, source_target_pairs={{0,10},{1,0},{2,24},{3,13},{4,26},{5,16},{6,29},{7,19},{8,1},{9,23... | collective-permute-start | bytes 110600 | tf_op jit(solution)/shard_map/ppermute | solution.py:385
  106.1 12.6 %collective-permute-start.39 = (f32[48,192]{1,0:T(8,128)S(1)}, f32[48,192]{1,0:T(8,128)S(1)}, u32[]{:S(2)}, u32[]{:S(2)}) collective-permute-start(f32[48,192]{1,0:T(8,128)S(1)} %get-tuple-element.91), channel_id=1, source_target_pairs={{0,21},{1,11},{2,2},{3,24},{4,16},{5,5},{6,8},{7,29},{8,12},{9,1},... | collective-permute-start | bytes 110600 | tf_op jit(solution)/shard_map/ppermute | solution.py:385
  111.4 0.7 copy-start.4
  113.8 7.0 %collective-permute-start.21 = (f32[192,128]{1,0:T(8,128)S(1)}, f32[192,128]{1,0:T(8,128)S(1)}, u32[]{:S(2)}, u32[]{:S(2)}) collective-permute-start(f32[192,128]{1,0:T(8,128)S(1)} %get-tuple-element.88), channel_id=1, source_target_pairs={{0,6},{1,7},{2,0},{3,1},{4,2},{5,3},{6,4},{7,5},{8,14},{9,15},{10,... | collective-permute-start | bytes 294920 | tf_op jit(solution)/shard_map/ppermute | solution.py:385
  115.8 26.1 %collective-permute-start.31 = (f32[392,128]{1,0:T(8,128)S(1)}, f32[392,128]{1,0:T(8,128)S(1)}, u32[]{:S(2)}, u32[]{:S(2)}) collective-permute-start(f32[392,128]{1,0:T(8,128)S(1)} %get-tuple-element.84), channel_id=1, source_target_pairs={{0,6},{1,7},{2,0},{3,1},{4,2},{5,3},{6,4},{7,5},{8,14},{9,15},{10,... | collective-permute-start | bytes 602120 | tf_op jit(solution)/shard_map/ppermute | solution.py:385
  116.7 25.2 %collective-permute-start.32 = (f32[392,128]{1,0:T(8,128)S(1)}, f32[392,128]{1,0:T(8,128)S(1)}, u32[]{:S(2)}, u32[]{:S(2)}) collective-permute-start(f32[392,128]{1,0:T(8,128)S(1)} %get-tuple-element.83), channel_id=1, source_target_pairs={{0,4},{1,5},{2,6},{3,7},{4,0},{5,1},{6,2},{7,3},{8,12},{9,13},{10,... | collective-permute-start | bytes 602120 | tf_op jit(solution)/shard_map/ppermute | solution.py:385
  118.7 23.1 %collective-permute-start.33 = (f32[392,128]{1,0:T(8,128)S(1)}, f32[392,128]{1,0:T(8,128)S(1)}, u32[]{:S(2)}, u32[]{:S(2)}) collective-permute-start(f32[392,128]{1,0:T(8,128)S(1)} %get-tuple-element.82), channel_id=1, source_target_pairs={{0,2},{1,3},{2,4},{3,5},{4,6},{5,7},{6,0},{7,1},{8,10},{9,11},{10,... | collective-permute-start | bytes 602120 | tf_op jit(solution)/shard_map/ppermute | solution.py:385
  118.7 22.3 %collective-permute-start.22 = (f32[192,128]{1,0:T(8,128)}, f32[192,128]{1,0:T(8,128)S(1)}, u32[]{:S(2)}, u32[]{:S(2)}) collective-permute-start(f32[192,128]{1,0:T(8,128)} %get-tuple-element.87), channel_id=1, source_target_pairs={{0,4},{1,5},{2,6},{3,7},{4,0},{5,1},{6,2},{7,3},{8,12},{9,13},{10,... | collective-permute-start | bytes 294920 | tf_op jit(solution)/shard_map/ppermute | solution.py:385
  120.9 20.1 %collective-permute-start.23 = (f32[192,128]{1,0:T(8,128)S(1)}, f32[192,128]{1,0:T(8,128)S(1)}, u32[]{:S(2)}, u32[]{:S(2)}) collective-permute-start(f32[192,128]{1,0:T(8,128)S(1)} %get-tuple-element.86), channel_id=1, source_target_pairs={{0,2},{1,3},{2,4},{3,5},{4,6},{5,7},{6,0},{7,1},{8,10},{9,11},{10,... | collective-permute-start | bytes 294920 | tf_op jit(solution)/shard_map/ppermute | solution.py:385
